TPU v7x, 512 devices: a whole 4x8x8 slice. The times are simulated.
512 devices in a mesh: grp: 8 (over y), tm: 64 (over z, x, core).
Axes of the slice: x: 4, y: 8, z: 8, core: 2. Of those that a mesh axis runs over, the one named last changes fastest.
Arguments:
- audio_rows: bfloat16 [131072, 1024], P(('grp', 'tm')), may hold values from -6 to 6
- routing: int32 [131072, 1], P(('grp', 'tm')), may hold values from 0 to 63; in each aligned block of 256 rows (0 to 255, 256 to 511, ...) at most 8 rows name the same one
- row_band: int32 [131072], P(('grp', 'tm')), may hold values from 0 to 3
- block_band: int32 [512], P(('grp', 'tm')), may hold values from 0 to 3
- latents: bfloat16 [65536, 1024], P(('grp', 'tm')), may hold values from -480 to 480
- kv_weight: bfloat16 [1024, 2048], P('tm'), may hold values from -0.1875 to 0.1875
- null_key: float32 [1024], replicated, may hold values from -6 to 6
- null_value: float32 [1024], replicated, may hold values from -6 to 6
- out_weight: bfloat16 [1024, 1024], replicated, may hold values from -0.1875 to 0.1875
- mlp_gain: float32 [1024], replicated, may hold values from 0.25 to 1.75
- up_weight: bfloat16 [1024, 8192], P('tm', 'grp'), may hold values from -0.1875 to 0.1875
- down_weight: bfloat16 [8192, 1024], P('grp', 'tm'), may hold values from -0.25 to 0.25
Outputs:
- mixed: bfloat16 [65536, 1024], P('tm', 'grp')
Inputs may be any that keep to these rules, and one draw needn't show every extreme that they name: `routing`: among the rows of one device no window is named by more than 8 rows, and in some devices' rows one window is named by exactly 8.
All inputs are finite; a program needn't handle non-finite values.
Results may differ from a plain program's by a relative error of at most 0.015.
Values may be sent and summed in bfloat16 or wider, within the bound.
No kernel may reach another device: no remote copies, remote signals or barrier semaphores. Data moves between devices by JAX's collectives and lax.ppermute only.
A program may use at most 64 MiB of HBM per device.

v0:
```python
import jax
import jax.numpy as jnp
from jax import lax
from jax.sharding import PartitionSpec as P

HD = 128


def attend(queries, kv_slots, usable, null_key, null_value):
    count = queries.shape[0]
    slots = kv_slots.shape[0]
    width = queries.shape[1]
    heads = width // HD
    scale = 1.0 / float(HD) ** 0.5
    query = queries.reshape(count, heads, HD)
    keyset = kv_slots[:, :width].reshape(slots, heads, HD)
    valset = kv_slots[:, width:].reshape(slots, heads, HD)
    scores = jnp.einsum("lhd,shd->hls", query, keyset, preferred_element_type=jnp.float32) * scale
    null_scores = (
        jnp.einsum("lhd,hd->hl", query.astype(jnp.float32), null_key.reshape(heads, HD)) * scale
    )
    masked = jnp.where(usable[None, None, :], scores, -1e30)
    highest = jnp.maximum(jnp.max(masked, axis=-1), null_scores)
    expo = jnp.where(usable[None, None, :], jnp.exp(masked - highest[:, :, None]), 0.0)
    null_expo = jnp.exp(null_scores - highest)
    denom = jnp.sum(expo, axis=-1) + null_expo
    weights = (expo / denom[:, :, None]).astype(jnp.bfloat16)
    null_weights = (null_expo / denom).astype(jnp.bfloat16)
    summed = jnp.einsum("hls,shd->lhd", weights, valset, preferred_element_type=jnp.float32)
    summed = (
        summed
        + jnp.transpose(null_weights.astype(jnp.float32))[:, :, None]
        * null_value.reshape(heads, HD)[None, :, :]
    )
    return summed.reshape(count, width).astype(jnp.bfloat16)


def local(
    audio_rows,
    routing,
    row_band,
    block_band,
    latents,
    kv_weight,
    null_key,
    null_value,
    out_weight,
    mlp_gain,
    up_weight,
    down_weight,
):
    local_rows = audio_rows.shape[0]
    owners = lax.axis_size("tm")
    capacity = max(2, 2 * local_rows // owners)
    destination = routing[:, 0]
    onehot = (destination[:, None] == jnp.arange(owners, dtype=jnp.int32)[None, :]).astype(
        jnp.int32
    )
    slot_index = jnp.sum((jnp.cumsum(onehot, axis=0) - onehot) * onehot, axis=1)
    band_send = (
        jnp.full((owners, capacity), -4, jnp.int32).at[destination, slot_index].set(row_band)
    )
    payload = (
        jnp.zeros((owners, capacity, audio_rows.shape[1]), jnp.bfloat16)
        .at[destination, slot_index]
        .set(audio_rows)
    )
    frame_recv, band_recv = (
        lax.all_to_all(payload, "tm", split_axis=0, concat_axis=0, tiled=True),
        lax.all_to_all(band_send, "tm", split_axis=0, concat_axis=0, tiled=True),
    )
    frame_slots = frame_recv.reshape(owners * capacity, audio_rows.shape[1])
    kv_whole = lax.all_gather(kv_weight, "tm", axis=0, tiled=True)
    kv_slots = jnp.dot(frame_slots, kv_whole, preferred_element_type=jnp.float32).astype(
        jnp.bfloat16
    )
    usable = jnp.abs(band_recv.reshape(-1) - block_band[0]) <= 1
    attended = attend(latents, kv_slots, usable, null_key, null_value)
    joined = (
        latents.astype(jnp.float32)
        + jnp.dot(attended, out_weight, preferred_element_type=jnp.float32)
    ).astype(jnp.bfloat16)
    window = lax.all_gather(joined, "grp", axis=0, tiled=True)
    values = window.astype(jnp.float32)
    center = values - jnp.mean(values, axis=-1, keepdims=True)
    spread = jnp.mean(center * center, axis=-1, keepdims=True)
    normed = (center * lax.rsqrt(spread + 1e-05) * mlp_gain).astype(jnp.bfloat16)
    up_whole = lax.all_gather(up_weight, "tm", axis=0, tiled=True)
    hidden = jax.nn.gelu(jnp.dot(normed, up_whole, preferred_element_type=jnp.float32)).astype(
        jnp.bfloat16
    )
    down_whole = lax.all_gather(down_weight, "tm", axis=1, tiled=True)
    partial_terms = jnp.dot(hidden, down_whole, preferred_element_type=jnp.float32)
    summed = lax.psum_scatter(
        partial_terms.astype(jnp.bfloat16), "grp", scatter_dimension=1, tiled=True
    ).astype(jnp.float32)
    columns = summed.shape[1]
    residual = lax.dynamic_slice_in_dim(window, lax.axis_index("grp") * columns, columns, 1)
    return (residual.astype(jnp.float32) + summed).astype(jnp.bfloat16)


def solution(mesh):
    return jax.shard_map(
        local,
        mesh=mesh,
        in_specs=(
            P(("grp", "tm"), None),
            P(("grp", "tm"), None),
            P(("grp", "tm")),
            P(("grp", "tm")),
            P(("grp", "tm"), None),
            P("tm", None),
            P(),
            P(),
            P(),
            P(),
            P("tm", "grp"),
            P("grp", "tm"),
        ),
        out_specs=P("tm", "grp"),
        check_vma=False,
    )
```

profile of v0, /device:TPU:4, one launch (start us, length us, event | category | flops | bytes accessed | tf_op | source)
XLA Modules:
  0.0 409.4 jit_solution(6860306548943538803)
XLA Ops:
  6.5 0.0 copy-start
  6.5 0.0 all-gather.5.cloned.1.call-start
  6.5 0.7 all-gather.5.cloned.1.call-update
  7.3 0.7 fusion.51
  8.0 0.6 reduce-window.6
  8.6 0.2 slice_reduce_fusion
  8.8 0.8 fusion.50
  9.6 0.7 or_select_fusion
  10.3 21.2 %scatter_fusion.1 = s32[64,8]{0,1:T(8,128)S(1)} fusion(s32[64,8]{0,1:T(8,128)S(1)} %broadcast_in_dim.40, s32[256]{0:T(256)S(1)} %bitcast.106, s32[256]{0:T(256)} %param.14), kind=kCustom, calls=%fused_computation.1 | custom fusion | bytes 5120 | tf_op jit(solution)/shard_map/scatter | solution.py:61
  31.6 0.7 copy.24
  32.3 13.8 %all-to-all-start.1 = ((s32[64,1,8]{2,1,0:T(1,128)}), s32[64,1,8]{2,1,0:T(1,128)S(1)}, u32[]{:S(2)}, u32[]{:S(2)}) async-start(s32[64,1,8]{2,1,0:T(1,128)} %copy.24), calls=%async_computation.1 | async-start | bytes 65536 | tf_op jit(solution)/shard_map/all_to_all | solution.py:70
  46.1 1.1 broadcast_in_dim.39
  47.2 0.0 copy-done.3
  47.2 36.1 %scatter_fusion = bf16[64,8,1024]{2,1,0:T(8,128)(2,1)} fusion(bf16[64,8,1024]{2,1,0:T(8,128)(2,1)} %broadcast_in_dim.39, s32[256]{0:T(256)S(1)} %bitcast.107, bf16[256,1024]{1,0:T(8,128)(2,1)S(1)} %copy-done.3), kind=kCustom, calls=%fused_computation | custom fusion | bytes 1574912 | tf_op jit(solution)/shard_map/scatter | solution.py:66
  83.4 0.0 all-to-all-done.1
  83.4 10.6 %all-to-all-start = ((bf16[64,8,1024]{2,1,0:T(8,128)(2,1)}), bf16[64,8,1024]{2,1,0:T(8,128)(2,1)S(1)}, u32[]{:S(2)}, u32[]{:S(2)}) async-start(bf16[64,8,1024]{2,1,0:T(8,128)(2,1)} %scatter_fusion), calls=%async_computation | async-start | bytes 2097152 | tf_op jit(solution)/shard_map/all_to_all | solution.py:69
  94.0 0.0 all-gather.7.cloned.1.call-start
  94.8 0.2 fusion.43
  95.0 0.2 compare_reduce_fusion
  95.1 0.1 le.15
  95.3 27.6 %all-to-all-done = bf16[64,8,1024]{2,1,0:T(8,128)(2,1)S(1)} async-done(((bf16[64,8,1024]{2,1,0:T(8,128)(2,1)}), bf16[64,8,1024]{2,1,0:T(8,128)(2,1)S(1)}, u32[]{:S(2)}, u32[]{:S(2)}) %all-to-all-start) | async-done | bytes 1048608 | tf_op jit(solution)/shard_map/all_to_all | solution.py:69
  122.8 4.5 %convolution_convert_fusion = bf16[512,2048]{1,0:T(8,128)(2,1)S(1)} fusion(bf16[1024,2048]{1,0:T(8,128)(2,1)} %all-gather.5.cloned.1.call-done, bf16[64,8,1024]{2,1,0:T(8,128)(2,1)S(1)} %all-to-all-done), kind=kOutput, calls=%fused_computation.18 | convolution fusion | flops 2148532224 | bytes 7340032 | tf_op jit(solution)/shard_map/dot_general | solution.py:74
  127.3 0.2 slice_bitcast_fusion
  127.6 0.5 bitcast_reduce_fusion
  128.1 1.3 copy-done.2
  129.4 0.6 fusion.29
  130.1 1.3 copy.32
  131.4 2.9 fusion.31
  134.3 1.2 fusion.32
  135.5 0.0 all-gather.7.cloned.1.call-update
  135.5 0.0 all-gather.11.cloned.1.call-start
  135.6 0.7 all-gather.11.cloned.1.call-update
  136.3 0.0 all-gather.9.cloned.1.call-start
  136.3 0.5 all-gather.9.cloned.1.call-update
  136.8 0.0 copy-start.7
  136.9 0.2 reduce-scatter.4.cloned.1.call-start
  137.1 38.1 %all-gather.7.cloned.1.call-done = bf16[1024,1024]{1,0:T(8,128)(2,1)} async-done(((bf16[128,1024]{1,0:T(8,128)(2,1)}), bf16[1024,1024]{1,0:T(8,128)(2,1)}) %all-gather.7.cloned.1.call-update) | async-done | bytes 2097168 | tf_op jit(solution)/shard_map/all_gather | solution.py:83
  175.2 2.1 convert_reduce_fusion
  177.3 0.1 copy-done.1
  177.4 0.7 fusion.2
  178.2 81.9 %all-gather.11.cloned.1.call-done = bf16[1024,1024]{0,1:T(8,128)(2,1)} async-done(((bf16[1024,16]{0,1:T(8,128)(2,1)}), bf16[1024,1024]{0,1:T(8,128)(2,1)}) %all-gather.11.cloned.1.call-update) | async-done | bytes 2097168 | tf_op jit(solution)/shard_map/all_gather | solution.py:92
  260.0 83.9 %all-gather.9.cloned.1.call-done = bf16[1024,1024]{1,0:T(8,128)(2,1)} async-done(((bf16[16,1024]{1,0:T(8,128)(2,1)}), bf16[1024,1024]{1,0:T(8,128)(2,1)}) %all-gather.9.cloned.1.call-update) | async-done | bytes 2097168 | tf_op jit(solution)/shard_map/all_gather | solution.py:88
  343.9 8.8 %fusion.26 = bf16[1024,1024]{1,0:T(8,128)(2,1)} fusion(bf16[1024,1024]{0,1:T(8,128)(2,1)} %all-gather.11.cloned.1.call-done, bf16[1024,1024]{1,0:T(8,128)(2,1)} %all-gather.9.cloned.1.call-done, bf16[1024,1024]{1,0:T(8,128)(2,1)} %all-gather.7.cloned.1.call-done, f32[1024]{0:T(1024)S(1)} %copy-done.7, f32[1024]{0:T(1024)S(1)} %add_rsqrt_fusion, ...), kind=kOutput, calls=%fused_computation.34 | convolution fusion | flops 4310695936 | bytes 8400896 | tf_op jit(solution)/shard_map/dot_general | solution.py:93
  352.7 3.9 copy.33
  356.7 0.0 reduce-scatter.4.cloned.1.call-update
  356.7 43.3 %reduce-scatter.4.cloned.1.call-done = bf16[128,1024]{1,0:T(8,128)(2,1)} async-done(((bf16[1024,1024]{1,0:T(8,128)(2,1)}), bf16[128,1024]{1,0:T(8,128)(2,1)}) %reduce-scatter.4.cloned.1.call-update) | async-done | bytes 262160
  400.0 1.1 copy.34
  401.1 1.7 add_convert_fusion
  (20 shorter events, 0.1 us)
Async XLA Ops:
  6.5 127.8 %copy-start = (bf16[1024,1024]{1,0:T(8,128)(2,1)S(1)}, bf16[1024,1024]{1,0:T(8,128)(2,1)}, u32[]{:S(2)}) copy-start(bf16[1024,1024]{1,0:T(8,128)(2,1)} %param.20) | copy-start | bytes 6291460
  6.5 40.7 %copy-start.3 = (bf16[256,1024]{1,0:T(8,128)(2,1)S(1)}, bf16[256,1024]{1,0:T(8,128)(2,1)}, u32[]{:S(2)}) copy-start(bf16[256,1024]{1,0:T(8,128)(2,1)} %param.12) | copy-start | bytes 1572868
  6.5 116.3 %all-gather.5.cloned.1.call-start = ((), (), s32[]{:S(2)}) async-start(), calls=%async_computation.3 | async-start | bytes 4259840 | tf_op jit(solution)/shard_map/all_gather | solution.py:73
  32.3 51.1 %all-to-all-start.1 = ((s32[64,1,8]{2,1,0:T(1,128)}), s32[64,1,8]{2,1,0:T(1,128)S(1)}, u32[]{:S(2)}, u32[]{:S(2)}) async-start(s32[64,1,8]{2,1,0:T(1,128)} %copy.24), calls=%async_computation.1 | async-start | bytes 65536 | tf_op jit(solution)/shard_map/all_to_all | solution.py:70
  83.4 11.4 %copy-start.4 = (bf16[128,1024]{1,0:T(8,128)(2,1)S(1)}, bf16[128,1024]{1,0:T(8,128)(2,1)}, u32[]{:S(2)}) copy-start(bf16[128,1024]{1,0:T(8,128)(2,1)} %param.16) | copy-start | bytes 786436
  83.4 11.4 %copy-start.5 = (f32[1024]{0:T(1024)S(1)}, f32[1024]{0:T(1024)}, u32[]{:S(2)}) copy-start(f32[1024]{0:T(1024)} %param.18) | copy-start | bytes 12292
  83.4 39.4 %all-to-all-start = ((bf16[64,8,1024]{2,1,0:T(8,128)(2,1)}), bf16[64,8,1024]{2,1,0:T(8,128)(2,1)S(1)}, u32[]{:S(2)}, u32[]{:S(2)}) async-start(bf16[64,8,1024]{2,1,0:T(8,128)(2,1)} %scatter_fusion), calls=%async_computation | async-start | bytes 2097152 | tf_op jit(solution)/shard_map/all_to_all | solution.py:69
  94.0 81.2 %all-gather.7.cloned.1.call-start = ((), (), s32[]{:S(2)}) async-start(), calls=%async_computation.4 | async-start | bytes 2359296 | tf_op jit(solution)/shard_map/all_gather | solution.py:83
  128.1 1.4 copy-start.2
  129.4 2.0 copy-start.6
  135.5 124.5 %all-gather.11.cloned.1.call-start = ((), (), s32[]{:S(2)}) async-start(), calls=%async_computation.6 | async-start | bytes 2129920 | tf_op jit(solution)/shard_map/all_gather | solution.py:92
  136.3 207.6 %all-gather.9.cloned.1.call-start = ((), (), s32[]{:S(2)}) async-start(), calls=%async_computation.5 | async-start | bytes 2129920 | tf_op jit(solution)/shard_map/all_gather | solution.py:88
  136.8 207.1 %copy-start.7 = (f32[1024]{0:T(1024)S(1)}, f32[1024]{0:T(1024)}, u32[]{:S(2)}) copy-start(f32[1024]{0:T(1024)} %param.21) | copy-start | bytes 12292
  136.9 263.1 %reduce-scatter.4.cloned.1.call-start = ((), (), s32[]{:S(2)}) async-start(), calls=%async_computation.7 | async-start | bytes 2359296
  175.2 2.2 copy-start.1
Sparse Core Ops, SparseCore 0:
  10.7 88.6 all-gather.4
  135.7 39.5 all-gather.6
  178.6 81.3 all-gather.10
  263.2 80.6 all-gather.8
  356.8 43.1 reduce-scatter.3
where the time goes:
time: 411 us; the launch traced here: 409 us
  waiting for transfers between devices  277 us (67%)
  local copies, waits for them, and re-layouts  67.6 us (16%)
  starting transfers between devices  24.8 us (6%)
  matrix products  18.1 us (4%)
  between operations  13.9 us (3%)
  other arithmetic  8.18 us (2%)
    all_gather x1, waiting for transfers between devices, local(): up_whole = lax.all_gather(up_weight, 'tm', axis=0, tiled=True)  83.9 us
    all_gather x1, waiting for transfers between devices, local(): down_whole = lax.all_gather(down_weight, 'tm', axis=1, tiled=True)  81.9 us
    unnamed x6, waiting for transfers between devices  45.3 us
    all_gather x1, waiting for transfers between devices, local(): window = lax.all_gather(joined, 'grp', axis=0, tiled=True)  38.1 us
    scatter x1, local copies, waits for them, and re-layouts, local(): payload = jnp.zeros((owners, capacity, audio_rows.shape[1]), jnp.bfloat16...  36.1 us
    all_to_all x1, waiting for transfers between devices, local(): lax.all_to_all(payload, 'tm', split_axis=0, concat_axis=0, tiled=True)  27.6 us
    scatter x1, local copies, waits for them, and re-layouts, local(): jnp.full((owners, capacity), -4, jnp.int32).at[destination, slot_index]  21.2 us
    all_to_all x1, starting transfers between devices, local(): lax.all_to_all(band_send, 'tm', split_axis=0, concat_axis=0, tiled=True)  13.8 us
  transfers between devices with their start and end apart: 7, of which 5 were waited for; matrix products, arithmetic and copies ran while one was open for 16% of the time, Pallas kernels for 0%

commit v1 on v0

--- a/solution.py
+++ b/solution.py
@@ -89,7 +89,10 @@
     hidden = jax.nn.gelu(jnp.dot(normed, up_whole, preferred_element_type=jnp.float32)).astype(
         jnp.bfloat16
     )
-    down_whole = lax.all_gather(down_weight, "tm", axis=1, tiled=True)
+    n_dev = lax.axis_size("tm")
+    pieces = jnp.stack([down_weight for _ in range(n_dev)])
+    pieces = lax.all_to_all(pieces, "tm", split_axis=0, concat_axis=0)
+    down_whole = jnp.concatenate(pieces, axis=1)
     partial_terms = jnp.dot(hidden, down_whole, preferred_element_type=jnp.float32)
     summed = lax.psum_scatter(
         partial_terms.astype(jnp.bfloat16), "grp", scatter_dimension=1, tiled=True

time: 411 us -> 328 us (0.80)
  the two profiles are of different devices: /device:TPU:4 before, /device:TPU:2 now
where the time goes in v1:
time: 328 us; the launch traced here: 326 us
  waiting for transfers between devices  185 us (56%)
  local copies, waits for them, and re-layouts  69.2 us (21%)
  starting transfers between devices  30.9 us (9%)
  matrix products  18.2 us (6%)
  between operations  14 us (4%)
  other arithmetic  8.18 us (2%)
    all_gather x1, waiting for transfers between devices, local(): up_whole = lax.all_gather(up_weight, 'tm', axis=0, tiled=True)  65.9 us
    unnamed x5, waiting for transfers between devices  44.7 us
    scatter x1, local copies, waits for them, and re-layouts, local(): payload = jnp.zeros((owners, capacity, audio_rows.shape[1]), jnp.bfloat16...  36.1 us
    all_gather x1, waiting for transfers between devices, local(): window = lax.all_gather(joined, 'grp', axis=0, tiled=True)  31 us
    all_to_all x1, waiting for transfers between devices, local(): lax.all_to_all(payload, 'tm', split_axis=0, concat_axis=0, tiled=True)  27.4 us
    scatter x1, local copies, waits for them, and re-layouts, local(): jnp.full((owners, capacity), -4, jnp.int32).at[destination, slot_index]  21.2 us
    all_to_all x1, waiting for transfers between devices, local(): pieces = lax.all_to_all(pieces, 'tm', split_axis=0, concat_axis=0)  16.3 us
    all_to_all x1, starting transfers between devices, local(): lax.all_to_all(band_send, 'tm', split_axis=0, concat_axis=0, tiled=True)  13.9 us
  transfers between devices with their start and end apart: 7, of which 5 were waited for; matrix products, arithmetic and copies ran while one was open for 21% of the time, Pallas kernels for 0%

profile of v1, /device:TPU:2, one launch (start us, length us, event | category | flops | bytes accessed | tf_op | source)
XLA Modules:
  0.0 325.6 jit_solution(16900585770056066666)
XLA Ops:
  6.5 0.7 all-gather.4.cloned.1.call-update
  7.3 0.7 fusion.51
  8.0 0.6 reduce-window.6
  8.6 0.2 slice_reduce_fusion
  8.8 0.8 fusion.50
  9.6 0.7 or_select_fusion
  10.3 21.2 %scatter_fusion.1 = s32[64,8]{0,1:T(8,128)S(1)} fusion(s32[64,8]{0,1:T(8,128)S(1)} %broadcast_in_dim.40, s32[256]{0:T(256)S(1)} %bitcast.109, s32[256]{0:T(256)} %param.14), kind=kCustom, calls=%fused_computation.1 | custom fusion | bytes 5120 | tf_op jit(solution)/shard_map/scatter | solution.py:61
  31.6 0.7 copy.25
  32.3 13.9 %all-to-all-start.1 = ((s32[64,1,8]{2,1,0:T(1,128)}), s32[64,1,8]{2,1,0:T(1,128)S(1)}, u32[]{:S(2)}, u32[]{:S(2)}) async-start(s32[64,1,8]{2,1,0:T(1,128)} %copy.25), calls=%async_computation.1 | async-start | bytes 65536 | tf_op jit(solution)/shard_map/all_to_all | solution.py:70
  46.2 1.1 broadcast_in_dim.39
  47.3 36.1 %scatter_fusion = bf16[64,8,1024]{2,1,0:T(8,128)(2,1)} fusion(bf16[64,8,1024]{2,1,0:T(8,128)(2,1)} %broadcast_in_dim.39, s32[256]{0:T(256)S(1)} %bitcast.110, bf16[256,1024]{1,0:T(8,128)(2,1)S(1)} %copy-done.3), kind=kCustom, calls=%fused_computation | custom fusion | bytes 1574912 | tf_op jit(solution)/shard_map/scatter | solution.py:66
  83.4 0.0 all-to-all-done.1
  83.4 10.7 %all-to-all-start = ((bf16[64,8,1024]{2,1,0:T(8,128)(2,1)}), bf16[64,8,1024]{2,1,0:T(8,128)(2,1)S(1)}, u32[]{:S(2)}, u32[]{:S(2)}) async-start(bf16[64,8,1024]{2,1,0:T(8,128)(2,1)} %scatter_fusion), calls=%async_computation | async-start | bytes 2097152 | tf_op jit(solution)/shard_map/all_to_all | solution.py:69
  94.1 0.0 all-gather.6.cloned.1.call-start
  94.8 0.0 copy-done.4
  94.8 0.0 copy-done.6
  94.8 0.2 fusion.43
  95.0 0.2 compare_reduce_fusion
  95.2 0.1 le.15
  95.3 27.4 %all-to-all-done = bf16[64,8,1024]{2,1,0:T(8,128)(2,1)S(1)} async-done(((bf16[64,8,1024]{2,1,0:T(8,128)(2,1)}), bf16[64,8,1024]{2,1,0:T(8,128)(2,1)S(1)}, u32[]{:S(2)}, u32[]{:S(2)}) %all-to-all-start) | async-done | bytes 1048608 | tf_op jit(solution)/shard_map/all_to_all | solution.py:69
  122.7 4.5 %convolution_convert_fusion = bf16[512,2048]{1,0:T(8,128)(2,1)S(1)} fusion(bf16[1024,2048]{1,0:T(8,128)(2,1)} %all-gather.4.cloned.1.call-done, bf16[64,8,1024]{2,1,0:T(8,128)(2,1)S(1)} %all-to-all-done), kind=kOutput, calls=%fused_computation.18 | convolution fusion | flops 2148532224 | bytes 7340032 | tf_op jit(solution)/shard_map/dot_general | solution.py:74
  127.2 0.2 slice_bitcast_fusion
  127.4 0.5 bitcast_reduce_fusion
  127.9 1.3 copy-done.2
  129.3 0.6 fusion.29
  129.9 1.3 copy.33
  131.3 2.9 fusion.31
  134.2 0.0 copy-start.5
  134.2 1.2 fusion.32
  135.4 0.0 all-gather.6.cloned.1.call-update
  135.4 1.6 stack.2
  137.0 6.0 %all-to-all-start.2 = ((bf16[64,1024,16]{1,2,0:T(8,128)(2,1)}), bf16[64,1024,16]{1,2,0:T(8,128)(2,1)}, u32[]{:S(2)}, u32[]{:S(2)}) async-start(bf16[64,1024,16]{1,2,0:T(8,128)(2,1)} %stack.2), calls=%async_computation.2 | async-start | bytes 4194304 | tf_op jit(solution)/shard_map/all_to_all | solution.py:94
  143.0 0.0 all-gather.8.cloned.1.call-start
  143.1 0.7 all-gather.8.cloned.1.call-update
  143.8 0.0 copy-start.8
  143.8 0.2 reduce-scatter.4.cloned.1.call-start
  144.0 31.0 %all-gather.6.cloned.1.call-done = bf16[1024,1024]{1,0:T(8,128)(2,1)} async-done(((bf16[128,1024]{1,0:T(8,128)(2,1)}), bf16[1024,1024]{1,0:T(8,128)(2,1)}) %all-gather.6.cloned.1.call-update) | async-done | bytes 2097168 | tf_op jit(solution)/shard_map/all_gather | solution.py:83
  175.0 2.1 convert_reduce_fusion
  177.1 0.1 copy-done.1
  177.2 0.7 fusion.2
  177.9 16.3 %all-to-all-done.2 = bf16[64,1024,16]{1,2,0:T(8,128)(2,1)} async-done(((bf16[64,1024,16]{1,2,0:T(8,128)(2,1)}), bf16[64,1024,16]{1,2,0:T(8,128)(2,1)}, u32[]{:S(2)}, u32[]{:S(2)}) %all-to-all-start.2) | async-done | bytes 2097184 | tf_op jit(solution)/shard_map/all_to_all | solution.py:94
  194.2 65.9 %all-gather.8.cloned.1.call-done = bf16[1024,1024]{1,0:T(8,128)(2,1)} async-done(((bf16[16,1024]{1,0:T(8,128)(2,1)}), bf16[1024,1024]{1,0:T(8,128)(2,1)}) %all-gather.8.cloned.1.call-update) | async-done | bytes 2097168 | tf_op jit(solution)/shard_map/all_gather | solution.py:88
  260.1 8.8 %fusion.26 = bf16[1024,1024]{1,0:T(8,128)(2,1)} fusion(bf16[1024,1024]{0,1:T(8,128)(2,1)} %bitcast.22, bf16[1024,1024]{1,0:T(8,128)(2,1)} %all-gather.8.cloned.1.call-done, bf16[1024,1024]{1,0:T(8,128)(2,1)} %all-gather.6.cloned.1.call-done, f32[1024]{0:T(1024)S(1)} %copy-done.8, f32[1024]{0:T(1024)S(1)} %add_rsqrt_fusion, f32[1024]{0:T(1024)S(1)} %broadcast_multiply_fusion), kind=kOutput, calls=%fused_computation.34 | convolution fusion | flops 4310695936 | bytes 8400896 | tf_op jit(solution)/shard_map/dot_general | solution.py:96
  268.9 4.0 %copy.34 = bf16[1024,1024]{0,1:T(8,128)(2,1)} copy(bf16[1024,1024]{1,0:T(8,128)(2,1)} %fusion.26) | data formatting | bytes 4194304
  272.9 0.0 reduce-scatter.4.cloned.1.call-update
  272.9 43.2 %reduce-scatter.4.cloned.1.call-done = bf16[128,1024]{1,0:T(8,128)(2,1)} async-done(((bf16[1024,1024]{1,0:T(8,128)(2,1)}), bf16[128,1024]{1,0:T(8,128)(2,1)}) %reduce-scatter.4.cloned.1.call-update) | async-done | bytes 262160
  316.2 1.1 copy.35
  317.3 1.7 add_convert_fusion
  (22 shorter events, 0.1 us)
Async XLA Ops:
  6.5 127.6 %copy-start = (bf16[1024,1024]{1,0:T(8,128)(2,1)S(1)}, bf16[1024,1024]{1,0:T(8,128)(2,1)}, u32[]{:S(2)}) copy-start(bf16[1024,1024]{1,0:T(8,128)(2,1)} %param.20) | copy-start | bytes 6291460
  6.5 40.7 %copy-start.3 = (bf16[256,1024]{1,0:T(8,128)(2,1)S(1)}, bf16[256,1024]{1,0:T(8,128)(2,1)}, u32[]{:S(2)}) copy-start(bf16[256,1024]{1,0:T(8,128)(2,1)} %param.12) | copy-start | bytes 1572868
  6.5 116.1 %all-gather.4.cloned.1.call-start = ((), (), s32[]{:S(2)}) async-start(), calls=%async_computation.4 | async-start | bytes 4259840 | tf_op jit(solution)/shard_map/all_gather | solution.py:73
  32.3 51.1 %all-to-all-start.1 = ((s32[64,1,8]{2,1,0:T(1,128)}), s32[64,1,8]{2,1,0:T(1,128)S(1)}, u32[]{:S(2)}, u32[]{:S(2)}) async-start(s32[64,1,8]{2,1,0:T(1,128)} %copy.25), calls=%async_computation.1 | async-start | bytes 65536 | tf_op jit(solution)/shard_map/all_to_all | solution.py:70
  83.4 11.4 %copy-start.4 = (bf16[128,1024]{1,0:T(8,128)(2,1)S(1)}, bf16[128,1024]{1,0:T(8,128)(2,1)}, u32[]{:S(2)}) copy-start(bf16[128,1024]{1,0:T(8,128)(2,1)} %param.16) | copy-start | bytes 786436
  83.4 11.4 %copy-start.6 = (f32[1024]{0:T(1024)S(1)}, f32[1024]{0:T(1024)}, u32[]{:S(2)}) copy-start(f32[1024]{0:T(1024)} %param.18) | copy-start | bytes 12292
  83.4 39.3 %all-to-all-start = ((bf16[64,8,1024]{2,1,0:T(8,128)(2,1)}), bf16[64,8,1024]{2,1,0:T(8,128)(2,1)S(1)}, u32[]{:S(2)}, u32[]{:S(2)}) async-start(bf16[64,8,1024]{2,1,0:T(8,128)(2,1)} %scatter_fusion), calls=%async_computation | async-start | bytes 2097152 | tf_op jit(solution)/shard_map/all_to_all | solution.py:69
  94.1 80.9 %all-gather.6.cloned.1.call-start = ((), (), s32[]{:S(2)}) async-start(), calls=%async_computation.5 | async-start | bytes 2359296 | tf_op jit(solution)/shard_map/all_gather | solution.py:83
  127.9 1.4 copy-start.2
  129.3 2.0 copy-start.7
  134.2 1.2 copy-start.5
  137.0 57.2 %all-to-all-start.2 = ((bf16[64,1024,16]{1,2,0:T(8,128)(2,1)}), bf16[64,1024,16]{1,2,0:T(8,128)(2,1)}, u32[]{:S(2)}, u32[]{:S(2)}) async-start(bf16[64,1024,16]{1,2,0:T(8,128)(2,1)} %stack.2), calls=%async_computation.2 | async-start | bytes 4194304 | tf_op jit(solution)/shard_map/all_to_all | solution.py:94
  143.0 117.1 %all-gather.8.cloned.1.call-start = ((), (), s32[]{:S(2)}) async-start(), calls=%async_computation.6 | async-start | bytes 2129920 | tf_op jit(solution)/shard_map/all_gather | solution.py:88
  143.8 116.3 %copy-start.8 = (f32[1024]{0:T(1024)S(1)}, f32[1024]{0:T(1024)}, u32[]{:S(2)}) copy-start(f32[1024]{0:T(1024)} %param.21) | copy-start | bytes 12292
  143.8 172.4 %reduce-scatter.4.cloned.1.call-start = ((), (), s32[]{:S(2)}) async-start(), calls=%async_computation.7 | async-start | bytes 2359296
  175.0 2.2 copy-start.1
Sparse Core Ops, SparseCore 0:
  10.7 89.1 all-gather.3
  135.5 39.4 all-gather.5
  178.3 81.7 all-gather.7
  273.0 43.0 reduce-scatter.3
